TPU v7x, 128 devices: a whole 4x4x4 slice. The times are simulated.
128 devices in a mesh: req: 16 (over z, x), tok: 8 (over y, core).
Axes of the slice: x: 4, y: 4, z: 4, core: 2. Of those that a mesh axis runs over, the one named last changes fastest.
Arguments:
- queries: bfloat16 [8192, 2048], P('req', 'tok'), may hold values from -6 to 6
- suffix_kv: bfloat16 [8192, 2048], P('req'), may hold values from -6 to 6
- prefix_cache: bfloat16 [8192, 2048], P('req'), may hold values from -24 to 24
- q_gain: float32 [256], replicated, may hold values from 0.1 to 1.9
- k_gain: float32 [256], replicated, may hold values from 0.1 to 1.9
- lengths: int32 [16, 3], P('req'), may hold values from 1 to 256, 512 in all within a row
- group_of: int32 [16], replicated, may hold values from 0 to 1
- owner_order: int32 [16], replicated, may hold values from 0 to 15, each once
- residual: bfloat16 [8192, 2560], P('req'), may hold values from -6 to 6
- w_out: bfloat16 [2048, 2560], P('tok'), may hold values from -0.125 to 0.125
- attn_gain: float32 [2560], replicated, may hold values from 0.1 to 1.9
- ffn_in_gain: float32 [2560], replicated, may hold values from 0.1 to 1.9
- ffn_out_gain: float32 [2560], replicated, may hold values from 0.1 to 1.9
- w_gate: bfloat16 [2560, 10240], P(None, 'tok'), may hold values from -0.125 to 0.125
- w_up: bfloat16 [2560, 10240], P(None, 'tok'), may hold values from -0.125 to 0.125
- w_down: bfloat16 [10240, 2560], P('tok'), may hold values from -0.0625 to 0.0625
Outputs:
- layer_out: bfloat16 [8192, 2560], P(('req', 'tok'))
Inputs may be any that keep to these rules, and one draw needn't show every extreme that they name: The 3 lengths of each req index sum to 512; the largest is exactly 256. `owner_order`: each req index appears once; entries g * 8 to g * 8 + 7 name the holders of group g's prefix.
All inputs are finite; a program needn't handle non-finite values.
Results may differ from a plain program's by a relative error of at most 0.02.
Values may be sent and summed in bfloat16 or wider, within the bound.
A program may use at most 128 MiB of HBM per device.

v0:
```python
import jax
import jax.numpy as jnp
from jax import lax
from jax.sharding import PartitionSpec as P

H = 8
KVH = 4
HD = 256
GROUPS = 2
EPSILON = 1e-06
MASKED = -1e30


def rms_scale(values_in, gain_vec):
    return (
        values_in
        * lax.rsqrt(jnp.mean(values_in * values_in, axis=-1, keepdims=True) + EPSILON)
        * gain_vec
    )


def norm_heads(values_in, gain_vec, head_count):
    row_count = values_in.shape[0]
    shaped = values_in.astype(jnp.float32).reshape(row_count, head_count, HD)
    return rms_scale(shaped, gain_vec).astype(jnp.bfloat16).reshape(row_count, head_count * HD)


def local(
    queries,
    suffix_kv,
    prefix_cache,
    q_gain,
    k_gain,
    lengths,
    group_of,
    owner_order,
    residual,
    w_out,
    attn_gain,
    ffn_in_gain,
    ffn_out_gain,
    w_gate,
    w_up,
    w_down,
):
    req_count = lax.axis_size("req")
    tok_count = lax.axis_size("tok")
    req_index = lax.axis_index("req")
    tok_index = lax.axis_index("tok")
    row_count = queries.shape[0]
    heads_here = queries.shape[1] // HD
    head_ratio = H // KVH
    kv_first = tok_index * heads_here // head_ratio
    kv_width = KVH * HD
    own_count = req_count // GROUPS
    with jax.named_scope("prefix_gather"):
        pref_keys = lax.dynamic_slice_in_dim(prefix_cache, kv_first * HD, HD, 1)
        pref_vals = lax.dynamic_slice_in_dim(prefix_cache, kv_width + kv_first * HD, HD, 1)
        pref_kv = jnp.concatenate([pref_keys, pref_vals], axis=1)
        half_rows = pref_kv.shape[0] // 2
        core = tok_index % 2
        my_half = lax.dynamic_slice_in_dim(pref_kv, core * half_rows, half_rows, 0)
        gathered = lax.all_gather(my_half, "req", axis=0, tiled=False)
        own_group = group_of[req_index]
        owner_ids = lax.dynamic_slice_in_dim(owner_order, own_group * own_count, own_count)
        picked = jnp.take(gathered, owner_ids, axis=0).reshape(-1, 2 * HD)
        partner = [(t, t ^ 1) for t in range(tok_count)]
        swapped = lax.ppermute(picked, "tok", perm=partner)
        shared = jnp.concatenate([picked, swapped], axis=0)
    with jax.named_scope("attention"):
        query_normed = norm_heads(queries, q_gain, heads_here)
        suf_keys = norm_heads(lax.dynamic_slice_in_dim(suffix_kv, kv_first * HD, HD, 1), k_gain, 1)
        suf_vals = lax.dynamic_slice_in_dim(suffix_kv, kv_width + kv_first * HD, HD, 1)
        all_keys = jnp.concatenate([shared[:, :HD], suf_keys], axis=0)
        all_vals = jnp.concatenate([shared[:, HD:], suf_vals], axis=0)
        seg_ends = jnp.cumsum(lengths[0])
        positions = jnp.arange(row_count, dtype=jnp.int32)
        segment = jnp.sum((positions[:, None] >= seg_ends[None, :]).astype(jnp.int32), axis=1)
        causal = (segment[:, None] == segment[None, :]) & (positions[None, :] <= positions[:, None])
        visible = jnp.concatenate(
            [jnp.ones((row_count, shared.shape[0]), jnp.bool_), causal], axis=1
        )
        outputs = []
        for head_idx in range(heads_here):
            head_q = query_normed[:, head_idx * HD : (head_idx + 1) * HD]
            scores = jnp.dot(head_q, all_keys.T, preferred_element_type=jnp.float32) * HD ** (-0.5)
            scores = jnp.where(visible, scores, MASKED)
            row_max = jnp.max(scores, axis=-1, keepdims=True)
            weights = jnp.exp(scores - row_max)
            row_sum = jnp.sum(weights, axis=-1, keepdims=True)
            head_out = (
                jnp.dot(weights.astype(jnp.bfloat16), all_vals, preferred_element_type=jnp.float32)
                / row_sum
            )
            outputs.append(head_out)
        attention = jnp.concatenate(outputs, axis=1).astype(jnp.bfloat16)
    share = row_count // tok_count
    first_row = tok_index * share
    with jax.named_scope("out_projection"):
        projected = lax.psum_scatter(
            jnp.dot(attention, w_out, preferred_element_type=jnp.float32).astype(jnp.bfloat16),
            "tok",
            scatter_dimension=0,
            tiled=True,
        )
        residual_share = lax.dynamic_slice_in_dim(residual, first_row, share, 0)
        mixed_share = residual_share.astype(jnp.float32) + rms_scale(
            projected.astype(jnp.float32), attn_gain
        )
        normed_share = rms_scale(mixed_share, ffn_in_gain).astype(jnp.bfloat16)
        normed = lax.all_gather(normed_share, "tok", axis=0, tiled=True)
    with jax.named_scope("feed_forward"):
        gate = jnp.dot(normed, w_gate, preferred_element_type=jnp.float32)
        upward = jnp.dot(normed, w_up, preferred_element_type=jnp.float32)
        hidden = (jax.nn.gelu(gate, approximate=True) * upward).astype(jnp.bfloat16)
        down_share = lax.psum_scatter(
            jnp.dot(hidden, w_down, preferred_element_type=jnp.float32).astype(jnp.bfloat16),
            "tok",
            scatter_dimension=0,
            tiled=True,
        )
    return (mixed_share + rms_scale(down_share.astype(jnp.float32), ffn_out_gain)).astype(
        jnp.bfloat16
    )


def solution(mesh):
    in_specs = (
        P("req", "tok"),
        P("req", None),
        P("req", None),
        P(),
        P(),
        P("req", None),
        P(),
        P(),
        P("req", None),
        P("tok", None),
        P(),
        P(),
        P(),
        P(None, "tok"),
        P(None, "tok"),
        P("tok", None),
    )
    out_specs = P(("req", "tok"), None)
    return jax.shard_map(local, mesh=mesh, in_specs=in_specs, out_specs=out_specs, check_vma=False)
```

profile of v0, /device:TPU:0, one launch (start us, length us, event | category | flops | bytes accessed | tf_op | source)
XLA Modules:
  0.0 226.1 jit_solution(17054381908956839786)
XLA Ops:
  6.5 1.2 constant_dynamic-slice_fusion.1
  7.7 0.7 fusion.49
  8.5 1.2 dynamic_slice.25
  10.4 0.7 compare_and_fusion
  11.1 0.1 broadcast_in_dim.20
  11.2 52.4 %all-gather.6.cloned.1.call-done = bf16[4096,512]{1,0:T(8,128)(2,1)} async-done(((bf16[256,512]{1,0:T(8,128)(2,1)}), bf16[4096,512]{1,0:T(8,128)(2,1)}) %all-gather.6.cloned.1.call-update) | async-done | bytes 4194320 | tf_op jit(solution)/shard_map/prefix_gather/all_gather | solution.py:63
  63.7 4.2 %gather_fusion = bf16[8,256,512]{2,1,0:T(8,128)(2,1)} fusion(bf16[16,256,512]{2,1,0:T(8,128)(2,1)} %bitcast.12, s32[1024]{0:T(1024)S(1)} %pad_clamp_fusion), kind=kCustom, calls=%fused_computation | custom fusion | bytes 4194336 | tf_op jit(solution)/shard_map/prefix_gather/jit(_take)/gather | solution.py:66
  67.9 1.8 bitcast_select_fusion
  69.7 0.1 collective-permute-start
  69.8 0.2 reduce-window.8
  69.9 1.1 fusion.46
  71.0 0.1 convert_reduce_fusion
  71.1 1.7 constant_dynamic-slice_fusion
  72.8 1.1 fusion.43
  73.9 1.1 fusion.48
  75.0 0.2 fusion.21
  75.3 1.4 fusion.20
  76.7 1.6 fusion.61
  78.3 3.6 %copy-done.1 = f32[512,4608]{1,0:T(8,128)} copy-done((f32[512,4608]{1,0:T(8,128)}, f32[512,4608]{1,0:T(8,128)S(1)}, u32[]{:S(2)}) %copy-start.1) | copy-done | bytes 9437208
  81.9 1.4 fusion
  83.3 8.9 %convolution_convert_fusion.1 = bf16[512,2560]{1,0:T(8,128)(2,1)} fusion(bf16[256,2560]{1,0:T(8,128)(2,1)S(1)} %copy-done, bf16[2048,512]{1,0:T(8,128)(2,1)} %collective-permute-done, bf16[2048,512]{1,0:T(8,128)(2,1)S(1)} %bitcast_select_fusion, bf16[512,256]{1,0:T(8,128)(2,1)} %constant_dynamic-slice_fusion, f32[512,4608]{1,0:T(8,128)} %copy-done.1, ...), kind=kOutput, calls=%fused_computation.8 | convolution fusion | flops 1892417536 | bytes 17829888 | tf_op jit(solution)/shard_map/out_projection/dot_general | solution.py:101
  92.3 34.4 %reduce-scatter.3.cloned.1.call-done = bf16[64,2560]{1,0:T(8,128)(2,1)} async-done(((bf16[512,2560]{1,0:T(8,128)(2,1)}), bf16[64,2560]{1,0:T(8,128)(2,1)}) %reduce-scatter.3.cloned.1.call-update) | async-done | bytes 327696 | tf_op jit(solution)/shard_map/out_projection/reduce_scatter | solution.py:100
  126.7 1.1 fusion.36
  127.9 1.4 multiply_reduce_fusion
  129.3 2.1 multiply_convert_fusion
  131.4 0.2 reduce-scatter.5.cloned.1.call-start
  131.6 24.9 %all-gather.4.cloned.1.call-done = bf16[512,2560]{1,0:T(8,128)(2,1)} async-done(((bf16[64,2560]{1,0:T(8,128)(2,1)}), bf16[512,2560]{1,0:T(8,128)(2,1)}) %all-gather.4.cloned.1.call-update) | async-done | bytes 2621456 | tf_op jit(solution)/shard_map/out_projection/all_gather | solution.py:111
  156.5 8.7 %fusion.62 = f32[512,1280]{1,0:T(8,128)} fusion(bf16[512,2560]{1,0:T(8,128)(2,1)} %all-gather.4.cloned.1.call-done, bf16[2560,1280]{1,0:T(8,128)(2,1)} %param.29), kind=kOutput, calls=%fused_computation.83 | convolution fusion | flops 3355443200 | bytes 11796480 | tf_op jit(solution)/shard_map/feed_forward/dot_general | solution.py:113
  165.2 15.6 %convolution_convert_fusion = bf16[512,2560]{1,0:T(8,128)(2,1)} fusion(bf16[1280,2560]{1,0:T(8,128)(2,1)} %param.31, bf16[512,2560]{1,0:T(8,128)(2,1)} %all-gather.4.cloned.1.call-done, bf16[2560,1280]{1,0:T(8,128)(2,1)} %param.30, f32[512,1280]{1,0:T(8,128)} %fusion.62), kind=kOutput, calls=%fused_computation.7 | convolution fusion | flops 6718750720 | bytes 20971520 | tf_op jit(solution)/shard_map/feed_forward/dot_general | solution.py:117
  180.9 35.3 %reduce-scatter.5.cloned.1.call-done = bf16[64,2560]{1,0:T(8,128)(2,1)} async-done(((bf16[512,2560]{1,0:T(8,128)(2,1)}), bf16[64,2560]{1,0:T(8,128)(2,1)}) %reduce-scatter.5.cloned.1.call-update) | async-done | bytes 327696 | tf_op jit(solution)/shard_map/feed_forward/reduce_scatter | solution.py:116
  216.2 1.1 fusion.39
  217.4 2.1 fusion.42
  (34 shorter events, 0.2 us)
Async XLA Ops:
  6.5 76.8 %copy-start = (bf16[256,2560]{1,0:T(8,128)(2,1)S(1)}, bf16[256,2560]{1,0:T(8,128)(2,1)}, u32[]{:S(2)}) copy-start(bf16[256,2560]{1,0:T(8,128)(2,1)} %param.25) | copy-start | bytes 3932164
  6.5 57.1 %all-gather.6.cloned.1.call-start = ((), (), s32[]{:S(2)}) async-start(), calls=%async_computation.5 | async-start | bytes 4456448 | tf_op jit(solution)/shard_map/prefix_gather/all_gather | solution.py:63
  8.5 118.3 %reduce-scatter.3.cloned.1.call-start = ((), (), s32[]{:S(2)}) async-start(), calls=%async_computation.2 | async-start | bytes 2949120 | tf_op jit(solution)/shard_map/out_projection/reduce_scatter | solution.py:100
  67.9 1.9 copy-start.9
  67.9 6.1 %copy-start.7 = (f32[256]{0:T(256)S(1)}, f32[256]{0:T(256)}, u32[]{:S(2)}) copy-start(f32[256]{0:T(256)} %param.20) | copy-start | bytes 3076
  69.7 5.6 %collective-permute-start = (bf16[2048,512]{1,0:T(8,128)(2,1)S(1)}, bf16[2048,512]{1,0:T(8,128)(2,1)}, u32[]{:S(2)}, u32[]{:S(2)}) collective-permute-start(bf16[2048,512]{1,0:T(8,128)(2,1)S(1)} %bitcast_select_fusion), channel_id=1, source_target_pairs={{0,1},{1,0},{2,3},{3,2},{4,5},{5,4},{6,7},{7,6},{8,9},{9,8},{10,11... | collective-permute-start | bytes 6291464 | tf_op jit(solution)/shard_map/prefix_gather/ppermute | solution.py:68
  75.2 1.4 copy-start.3
  75.3 1.4 copy-start.8
  78.3 3.6 %copy-start.1 = (f32[512,4608]{1,0:T(8,128)}, f32[512,4608]{1,0:T(8,128)S(1)}, u32[]{:S(2)}) copy-start(f32[512,4608]{1,0:T(8,128)S(1)} %get-tuple-element.10) | copy-start | bytes 28311556
  92.2 35.7 %copy-start.4 = (f32[2560]{0:T(1024)S(1)}, f32[2560]{0:T(1024)}, u32[]{:S(2)}) copy-start(f32[2560]{0:T(1024)} %param.26) | copy-start | bytes 30724
  92.2 37.1 %copy-start.5 = (f32[2560]{0:T(1024)S(1)}, f32[2560]{0:T(1024)}, u32[]{:S(2)}) copy-start(f32[2560]{0:T(1024)} %param.27) | copy-start | bytes 30724
  92.2 64.3 %all-gather.4.cloned.1.call-start = ((), (), s32[]{:S(2)}) async-start(), calls=%async_computation.3 | async-start | bytes 2949120 | tf_op jit(solution)/shard_map/out_projection/all_gather | solution.py:111
  131.4 84.8 %reduce-scatter.5.cloned.1.call-start = ((), (), s32[]{:S(2)}) async-start(), calls=%async_computation.4 | async-start | bytes 2949120 | tf_op jit(solution)/shard_map/feed_forward/reduce_scatter | solution.py:116
  180.9 36.5 %copy-start.2 = (bf16[64,2560]{1,0:T(8,128)(2,1)S(1)}, bf16[64,2560]{1,0:T(8,128)(2,1)}, u32[]{:S(2)}) copy-start(bf16[64,2560]{1,0:T(8,128)(2,1)} %reduce-scatter.3.cloned.1.call-done) | copy-start | bytes 983044
  180.9 36.5 %copy-start.6 = (f32[2560]{0:T(1024)S(1)}, f32[2560]{0:T(1024)}, u32[]{:S(2)}) copy-start(f32[2560]{0:T(1024)} %param.28) | copy-start | bytes 30724
Sparse Core Ops, SparseCore 0:
  9.5 54.1 all-gather.5
  92.3 34.3 reduce-scatter.2
  131.5 24.9 all-gather.3
  181.0 35.1 reduce-scatter.4
where the time goes:
time: 227 us; the launch traced here: 226 us
  waiting for transfers between devices  147 us (65%)
  matrix products  34.8 us (15%)
  other arithmetic  17.7 us (8%)
  between operations  14 us (6%)
  local copies, waits for them, and re-layouts  12 us (5%)
    all_gather x1, waiting for transfers between devices, local(): gathered = lax.all_gather(my_half, 'req', axis=0, tiled=False)  52.4 us
    reduce_scatter x1, waiting for transfers between devices, local(): lax.psum_scatter(jnp.dot(hidden, w_down, preferred_element_type=jnp.float...  35.3 us
    reduce_scatter x1, waiting for transfers between devices, local(): lax.psum_scatter(jnp.dot(attention, w_out, preferred_element_type=jnp.flo...  34.4 us
    all_gather x1, waiting for transfers between devices, local(): normed = lax.all_gather(normed_share, 'tok', axis=0, tiled=True)  24.9 us
    dot_general x1, matrix products, local(): jnp.dot(hidden, w_down, preferred_element_type=jnp.float32)  15.6 us
    dot_general x1, matrix products, local(): jnp.dot(attention, w_out, preferred_element_type=jnp.float32)  8.88 us
    dot_general x1, matrix products, local(): gate = jnp.dot(normed, w_gate, preferred_element_type=jnp.float32)  8.71 us
    reduce_sum x5, other arithmetic, rms_scale(): jnp.mean(values_in * values_in, axis=-1, keepdims=True) + EPSILON  5.86 us
  transfers between devices with their start and end apart: 5, of which 4 were waited for; matrix products, arithmetic and copies ran while one was open for 3% of the time, Pallas kernels for 0%

commit v1 on v0

--- a/solution.py
+++ b/solution.py
@@ -108,7 +108,8 @@
             projected.astype(jnp.float32), attn_gain
         )
         normed_share = rms_scale(mixed_share, ffn_in_gain).astype(jnp.bfloat16)
-        normed = lax.all_gather(normed_share, "tok", axis=0, tiled=True)
+        sent = jnp.stack([normed_share] * lax.axis_size("tok"))
+        normed = jnp.concatenate(lax.all_to_all(sent, "tok", 0, 0), axis=0)
     with jax.named_scope("feed_forward"):
         gate = jnp.dot(normed, w_gate, preferred_element_type=jnp.float32)
         upward = jnp.dot(normed, w_up, preferred_element_type=jnp.float32)

time: 227 us -> 236 us (1.040)
  blocking collectives: 0 us -> 35.7 us
  waiting for transfers between devices: 147 us -> 121 us
    all_to_all x0 -> x1, blocking collectives: none -> 35.7 us  [local(): normed = jnp.concatenate(lax.all_to_all(sent, 'tok', 0, 0), axis=0)]
    all_gather x1 -> x0, waiting for transfers between devices: 24.9 us -> none  [local(): normed = lax.all_gather(normed_share, 'tok', axis=0, tiled=True)]
    unnamed x20 -> x22, local copies, waits for them, and re-layouts: 3.66 us -> 5.19 us
  transfers between devices with their start and end apart: 5 -> 4, of which waited for: 4 -> 3; matrix products, arithmetic and copies ran while one was open for 3% -> 3% of each run, Pallas kernels for 0% -> 0%
where the time goes in v1:
time: 236 us
  waiting for transfers between devices  121 us (51%)
  blocking collectives  35.7 us (15%)
  matrix products  34 us (14%)
  other arithmetic  17 us (7%)
  between operations  14 us (6%)
  local copies, waits for them, and re-layouts  13.8 us (6%)
    all_gather x1, waiting for transfers between devices, local(): gathered = lax.all_gather(my_half, 'req', axis=0, tiled=False)  52.4 us
    all_to_all x1, blocking collectives, local(): normed = jnp.concatenate(lax.all_to_all(sent, 'tok', 0, 0), axis=0)  35.7 us
    reduce_scatter x1, waiting for transfers between devices, local(): lax.psum_scatter(jnp.dot(attention, w_out, preferred_element_type=jnp.flo...  34.4 us
    reduce_scatter x1, waiting for transfers between devices, local(): lax.psum_scatter(jnp.dot(hidden, w_down, preferred_element_type=jnp.float...  34.2 us
    dot_general x1, matrix products, local(): jnp.dot(hidden, w_down, preferred_element_type=jnp.float32)  15.6 us
    dot_general x1, matrix products, local(): jnp.dot(attention, w_out, preferred_element_type=jnp.float32)  8.88 us
    dot_general x1, matrix products, local(): gate = jnp.dot(normed, w_gate, preferred_element_type=jnp.float32)  7.91 us
    reduce_sum x5, other arithmetic, rms_scale(): jnp.mean(values_in * values_in, axis=-1, keepdims=True) + EPSILON  5.86 us
  transfers between devices with their start and end apart: 4, of which 3 were waited for; matrix products, arithmetic and copies ran while one was open for 3% of the time, Pallas kernels for 0%

profile of v1, /device:TPU:0, one launch (start us, length us, event | category | flops | bytes accessed | tf_op | source)
XLA Modules:
  0.0 235.7 jit_solution(7091049655828218072)
XLA Ops:
  6.5 1.2 constant_dynamic-slice_fusion.1
  7.7 0.7 fusion.49
  8.5 1.2 dynamic_slice.25
  10.4 0.7 compare_and_fusion
  11.2 52.4 %all-gather.3.cloned.1.call-done = bf16[4096,512]{1,0:T(8,128)(2,1)} async-done(((bf16[256,512]{1,0:T(8,128)(2,1)}), bf16[4096,512]{1,0:T(8,128)(2,1)}) %all-gather.3.cloned.1.call-update) | async-done | bytes 4194320 | tf_op jit(solution)/shard_map/prefix_gather/all_gather | solution.py:63
  63.7 4.2 %gather_fusion = bf16[8,256,512]{2,1,0:T(8,128)(2,1)} fusion(bf16[16,256,512]{2,1,0:T(8,128)(2,1)} %bitcast.15, s32[1024]{0:T(1024)S(1)} %pad_clamp_fusion), kind=kCustom, calls=%fused_computation | custom fusion | bytes 4194336 | tf_op jit(solution)/shard_map/prefix_gather/jit(_take)/gather | solution.py:66
  67.9 1.8 bitcast_select_fusion
  69.7 0.1 collective-permute-start
  69.8 0.2 reduce-window.8
  69.9 1.1 fusion.46
  71.0 0.1 convert_reduce_fusion
  71.1 1.7 constant_dynamic-slice_fusion
  72.8 1.1 fusion.43
  73.9 1.1 fusion.48
  75.0 0.2 fusion.21
  75.3 1.4 fusion.20
  76.7 1.6 fusion.61
  78.3 3.6 %copy-done.1 = f32[512,4608]{1,0:T(8,128)} copy-done((f32[512,4608]{1,0:T(8,128)}, f32[512,4608]{1,0:T(8,128)S(1)}, u32[]{:S(2)}) %copy-start.1) | copy-done | bytes 9437208
  81.9 1.4 fusion
  83.3 8.9 %convolution_convert_fusion.1 = bf16[512,2560]{1,0:T(8,128)(2,1)} fusion(bf16[256,2560]{1,0:T(8,128)(2,1)S(1)} %copy-done, bf16[2048,512]{1,0:T(8,128)(2,1)} %collective-permute-done, bf16[2048,512]{1,0:T(8,128)(2,1)S(1)} %bitcast_select_fusion, bf16[512,256]{1,0:T(8,128)(2,1)} %constant_dynamic-slice_fusion, f32[512,4608]{1,0:T(8,128)} %copy-done.1, ...), kind=kOutput, calls=%fused_computation.8 | convolution fusion | flops 1892417536 | bytes 17829888 | tf_op jit(solution)/shard_map/out_projection/dot_general | solution.py:101
  92.3 34.4 %reduce-scatter.3.cloned.1.call-done = bf16[64,2560]{1,0:T(8,128)(2,1)} async-done(((bf16[512,2560]{1,0:T(8,128)(2,1)}), bf16[64,2560]{1,0:T(8,128)(2,1)}) %reduce-scatter.3.cloned.1.call-update) | async-done | bytes 327696 | tf_op jit(solution)/shard_map/out_projection/reduce_scatter | solution.py:100
  126.7 1.1 fusion.36
  127.9 1.4 multiply_reduce_fusion
  129.3 1.3 multiply_convert_fusion
  130.6 0.2 stack.2
  130.9 35.7 %all_to_all.5 = bf16[8,64,2560]{2,1,0:T(8,128)(2,1)S(1)} all-to-all(bf16[8,64,2560]{2,1,0:T(8,128)(2,1)S(1)} %stack.2), channel_id=1, replica_groups=mesh['req'=16,'tok'=8] {'tok'}, dimensions={0} | all-to-all | bytes 5242880 | tf_op jit(solution)/shard_map/out_projection/all_to_all | solution.py:112
  166.5 1.5 copy-done.3
  168.1 7.9 %fusion.62 = f32[512,1280]{1,0:T(8,128)} fusion(bf16[512,2560]{1,0:T(8,128)(2,1)S(1)} %bitcast.13, bf16[2560,1280]{1,0:T(8,128)(2,1)} %param.29), kind=kOutput, calls=%fused_computation.83 | convolution fusion | flops 3355443200 | bytes 11796480 | tf_op jit(solution)/shard_map/feed_forward/dot_general | solution.py:114
  176.0 15.6 %convolution_convert_fusion = bf16[512,2560]{1,0:T(8,128)(2,1)} fusion(bf16[1280,2560]{1,0:T(8,128)(2,1)} %param.31, bf16[512,2560]{1,0:T(8,128)(2,1)} %bitcast.14, bf16[2560,1280]{1,0:T(8,128)(2,1)} %param.30, f32[512,1280]{1,0:T(8,128)} %fusion.62), kind=kOutput, calls=%fused_computation.7 | convolution fusion | flops 6718750720 | bytes 20971520 | tf_op jit(solution)/shard_map/feed_forward/dot_general | solution.py:118
  191.6 34.2 %reduce-scatter.5.cloned.1.call-done = bf16[64,2560]{1,0:T(8,128)(2,1)} async-done(((bf16[512,2560]{1,0:T(8,128)(2,1)}), bf16[64,2560]{1,0:T(8,128)(2,1)}) %reduce-scatter.5.cloned.1.call-update) | async-done | bytes 327696 | tf_op jit(solution)/shard_map/feed_forward/reduce_scatter | solution.py:117
  225.9 1.1 fusion.39
  227.0 2.1 fusion.42
  (35 shorter events, 0.3 us)
Async XLA Ops:
  6.5 76.8 %copy-start = (bf16[256,2560]{1,0:T(8,128)(2,1)S(1)}, bf16[256,2560]{1,0:T(8,128)(2,1)}, u32[]{:S(2)}) copy-start(bf16[256,2560]{1,0:T(8,128)(2,1)} %param.25) | copy-start | bytes 3932164
  6.5 57.1 %all-gather.3.cloned.1.call-start = ((), (), s32[]{:S(2)}) async-start(), calls=%async_computation.5 | async-start | bytes 4456448 | tf_op jit(solution)/shard_map/prefix_gather/all_gather | solution.py:63
  8.5 118.3 %reduce-scatter.3.cloned.1.call-start = ((), (), s32[]{:S(2)}) async-start(), calls=%async_computation.3 | async-start | bytes 2949120 | tf_op jit(solution)/shard_map/out_projection/reduce_scatter | solution.py:100
  67.9 1.9 copy-start.10
  67.9 6.1 %copy-start.8 = (f32[256]{0:T(256)S(1)}, f32[256]{0:T(256)}, u32[]{:S(2)}) copy-start(f32[256]{0:T(256)} %param.20) | copy-start | bytes 3076
  69.7 5.6 %collective-permute-start = (bf16[2048,512]{1,0:T(8,128)(2,1)S(1)}, bf16[2048,512]{1,0:T(8,128)(2,1)}, u32[]{:S(2)}, u32[]{:S(2)}) collective-permute-start(bf16[2048,512]{1,0:T(8,128)(2,1)S(1)} %bitcast_select_fusion), channel_id=1, source_target_pairs={{0,1},{1,0},{2,3},{3,2},{4,5},{5,4},{6,7},{7,6},{8,9},{9,8},{10,11... | collective-permute-start | bytes 6291464 | tf_op jit(solution)/shard_map/prefix_gather/ppermute | solution.py:68
  75.2 1.4 copy-start.4
  75.3 1.4 copy-start.9
  78.3 3.6 %copy-start.1 = (f32[512,4608]{1,0:T(8,128)}, f32[512,4608]{1,0:T(8,128)S(1)}, u32[]{:S(2)}) copy-start(f32[512,4608]{1,0:T(8,128)S(1)} %get-tuple-element.10) | copy-start | bytes 28311556
  92.2 35.7 %copy-start.5 = (f32[2560]{0:T(1024)S(1)}, f32[2560]{0:T(1024)}, u32[]{:S(2)}) copy-start(f32[2560]{0:T(1024)} %param.26) | copy-start | bytes 30724
  92.2 37.1 %copy-start.6 = (f32[2560]{0:T(1024)S(1)}, f32[2560]{0:T(1024)}, u32[]{:S(2)}) copy-start(f32[2560]{0:T(1024)} %param.27) | copy-start | bytes 30724
  92.2 133.6 %reduce-scatter.5.cloned.1.call-start = ((), (), s32[]{:S(2)}) async-start(), calls=%async_computation.4 | async-start | bytes 2949120 | tf_op jit(solution)/shard_map/feed_forward/reduce_scatter | solution.py:117
  166.5 1.5 copy-start.3
  191.6 35.4 %copy-start.2 = (bf16[64,2560]{1,0:T(8,128)(2,1)S(1)}, bf16[64,2560]{1,0:T(8,128)(2,1)}, u32[]{:S(2)}) copy-start(bf16[64,2560]{1,0:T(8,128)(2,1)} %reduce-scatter.3.cloned.1.call-done) | copy-start | bytes 983044
  191.6 35.4 %copy-start.7 = (f32[2560]{0:T(1024)S(1)}, f32[2560]{0:T(1024)}, u32[]{:S(2)}) copy-start(f32[2560]{0:T(1024)} %param.28) | copy-start | bytes 30724
Sparse Core Ops, SparseCore 0:
  9.5 54.1 all-gather.2
  92.3 34.3 reduce-scatter.2
  191.8 34.0 reduce-scatter.4
